TPU v7x, 128 devices: a whole 4x4x4 slice. The times are simulated.
128 devices in a mesh: expert: 8 (over y, z_lo), shard: 16 (over z_hi, x, core).
Axes of the slice: x: 4, y: 4, z: 4 (z_hi: 2, z_lo: 2; z = z_hi * 2 + z_lo), core: 2. Of those that a mesh axis runs over, the one named last changes fastest.
Arguments:
- pre_hidden: bfloat16 [7680, 4096], P(('expert', 'shard')), may hold values from -12 to 12
- dec_resid: bfloat16 [16, 32, 4096], P('shard', 'expert'), may hold values from -12 to 12
- dec_query: bfloat16 [512, 4096], P('shard', 'expert'), may hold values from -4.5 to 4.5
- kv_pool: bfloat16 [8, 16896, 16, 256], P('expert', 'shard'), may hold values from -4.5 to 4.5
- page_table: int32 [16, 32, 128], P('shard'), may hold values from 0 to 1055, as said below
- cache_len: int32 [16, 32], P('shard'), may hold values from 2 to 2048, as said below
- out_weight: bfloat16 [4096, 4096], P('expert'), may hold values from -0.5 to 0.5
- norm_gain: float32 [4096], replicated, may hold values from 0.5 to 1.5
- route_ids_pre: int32 [7680, 2], P(('expert', 'shard')), may hold values from 0 to 7, as said below
- route_ids_dec: int32 [16, 32, 2], P('shard', 'expert'), may hold values from 0 to 7, as said below
- route_logit_pre: float32 [7680, 2], P(('expert', 'shard')), may hold values from -6 to 6
- route_logit_dec: float32 [16, 32, 2], P('shard', 'expert'), may hold values from -6 to 6
- expert_slot: int32 [8], replicated, may hold values from 0 to 7, each once
- w_gate: bfloat16 [8, 4096, 8192], P('expert', None, 'shard'), may hold values from -0.09375 to 0.09375
- w_up: bfloat16 [8, 4096, 8192], P('expert', None, 'shard'), may hold values from -0.09375 to 0.09375
- w_down: bfloat16 [8, 8192, 4096], P('expert', 'shard'), may hold values from -0.0625 to 0.0625
Outputs:
- mixed_pre: bfloat16 [7680, 4096], P(('expert', 'shard'))
- mixed_dec: bfloat16 [16, 32, 4096], P('shard', 'expert')
Inputs may be any that keep to these rules, and one draw needn't show every extreme that they name: `cache_len`: the requests of one shard index hold at most 16384 cached positions together, and one of them holds exactly 2048. `page_table`: for request i of shard index s, entries j below ceil(cache_len[s, i] / 16) name pages of the pool of that shard index, all distinct over the shard index; the other entries are unused. `route_ids_pre`: each row names two different experts. The rows of one device (its 60 prefill rows and its 4 decode rows) name each expert at most 18 times, and some expert exactly 18 times on every device. `route_ids_dec`: as for route_ids_pre: a device's decode rows count with its prefill rows.
All inputs are finite; a program needn't handle non-finite values.
Results may differ from a plain program's by a relative error of at most 0.015.
Values may be sent and summed in bfloat16 or wider, within the bound.
A program may use at most 192 MiB of HBM per device.

v0:
```python
import jax
import jax.numpy as jnp
from jax import lax
from jax.sharding import PartitionSpec as P


def table_attention(dec_query, kv_pool, page_rows, lengths):
    dec_dev, local_cols = dec_query.shape
    kv_local, pool_dev, page_size, twice_dim = kv_pool.shape
    head_dim = twice_dim // 2
    group_size = local_cols // (head_dim * kv_local)
    span_tokens = page_rows.shape[1] * page_size
    queries = dec_query.reshape(dec_dev, kv_local, group_size, head_dim)
    gathered = kv_pool[:, page_rows].reshape(kv_local, dec_dev, span_tokens, twice_dim)
    scores = jnp.einsum(
        "rkgd,krtd->rkgt", queries, gathered[..., :head_dim], preferred_element_type=jnp.float32
    ) * head_dim ** (-0.5)
    live_pos = (jnp.arange(span_tokens, dtype=jnp.int32)[None, :] < lengths[:, None])[
        :, None, None, :
    ]
    row_top = jnp.max(jnp.where(live_pos, scores, -jnp.inf), axis=-1, keepdims=True)
    weights_f = jnp.where(live_pos, jnp.exp(scores - row_top), 0.0)
    totals = jnp.sum(weights_f, axis=-1)
    weights_b = weights_f.astype(jnp.bfloat16)
    summed = jnp.einsum(
        "rkgt,krtd->rkgd", weights_b, gathered[..., head_dim:], preferred_element_type=jnp.float32
    )
    return (summed / totals[..., None]).astype(jnp.bfloat16).reshape(dec_dev, local_cols)


def local(
    pre_hidden,
    dec_resid,
    dec_query,
    kv_pool,
    page_table,
    cache_len,
    out_weight,
    norm_gain,
    route_ids_pre,
    route_ids_dec,
    route_logit_pre,
    route_logit_dec,
    expert_slot,
    w_gate,
    w_up,
    w_down,
):
    n_expert = lax.axis_size("expert")
    page_rows = page_table[0]
    lengths = cache_len[0]
    attn = table_attention(dec_query, kv_pool, page_rows, lengths)
    head_total = lax.psum_scatter(
        jnp.dot(attn, out_weight, preferred_element_type=jnp.float32).astype(jnp.bfloat16),
        "expert",
        scatter_dimension=0,
        tiled=True,
    ).astype(jnp.float32)
    h_dec = (dec_resid[0].astype(jnp.float32) + head_total).astype(jnp.bfloat16)
    hidden = jnp.concatenate([pre_hidden, h_dec], axis=0)
    route_ids = jnp.concatenate([route_ids_pre, route_ids_dec[0]], axis=0)
    logits = jnp.concatenate([route_logit_pre, route_logit_dec[0]], axis=0)
    pre_count = pre_hidden.shape[0]
    rows_dev, width = hidden.shape
    slot_cap = (rows_dev + 3) // 4 + 2
    stream = hidden.astype(jnp.float32)
    normed = (
        stream * lax.rsqrt(jnp.mean(stream * stream, axis=-1, keepdims=True) + 1e-05) * norm_gain
    ).astype(jnp.bfloat16)
    shares = jnp.stack(
        [jax.nn.sigmoid(logits[:, 0] - logits[:, 1]), jax.nn.sigmoid(logits[:, 1] - logits[:, 0])],
        axis=-1,
    )
    experts = expert_slot.shape[0]
    per_group = w_gate.shape[0]
    expert_ids = jnp.arange(experts, dtype=jnp.int32)
    slot_match = expert_slot[None, :] == expert_ids[:, None]
    slot_of = jnp.sum(jnp.where(slot_match, expert_ids[None, :], 0), axis=1)
    slot_ids = jnp.sum(jnp.where(route_ids[..., None] == expert_ids, slot_of, 0), axis=-1)
    flat_slots = slot_ids.reshape(-1)
    slot_hot = (flat_slots[:, None] == expert_ids[None, :]).astype(jnp.int32)
    ranking = jnp.sum((jnp.cumsum(slot_hot, axis=0) - slot_hot) * slot_hot, axis=1)
    slot_pos = (flat_slots * slot_cap + ranking).reshape(rows_dev, 2)
    slots_all = experts * slot_cap
    placing = jnp.any(
        jnp.arange(slots_all, dtype=jnp.int32)[:, None, None] == slot_pos[None], axis=-1
    ).astype(jnp.bfloat16)
    buffer = jnp.dot(placing, normed, preferred_element_type=jnp.float32).astype(jnp.bfloat16)
    buffer = buffer.reshape(n_expert, per_group, slot_cap, width)
    received = lax.all_to_all(buffer, "expert", split_axis=0, concat_axis=0, tiled=True)
    piece_rows = lax.all_gather(received[None], "shard", axis=0, tiled=True)
    gate = jnp.einsum("sgkcd,kdf->sgkcf", piece_rows, w_gate, preferred_element_type=jnp.float32)
    upper = jnp.einsum("sgkcd,kdf->sgkcf", piece_rows, w_up, preferred_element_type=jnp.float32)
    act = (jax.nn.silu(gate) * upper).astype(jnp.bfloat16)
    term = jnp.einsum("sgkcf,kfd->sgkcd", act, w_down, preferred_element_type=jnp.float32)
    own_rows = lax.psum_scatter(
        term.astype(jnp.bfloat16).astype(jnp.float32).astype(jnp.bfloat16),
        "shard",
        scatter_dimension=0,
        tiled=True,
    ).astype(jnp.float32)
    outputs = own_rows[0].astype(jnp.bfloat16)
    returned = lax.all_to_all(outputs, "expert", split_axis=0, concat_axis=0, tiled=True).reshape(
        slots_all, width
    )
    picked = returned[slot_pos]
    mixed_rows = stream + jnp.sum(shares[..., None] * picked.astype(jnp.float32), axis=1)
    mixed_out = mixed_rows.astype(jnp.bfloat16)
    return (mixed_out[:pre_count], mixed_out[pre_count:][None])


def solution(mesh):
    placed = (
        P(("expert", "shard"), None),
        P("shard", "expert", None),
        P("shard", "expert"),
        P("expert", "shard", None, None),
        P("shard", None, None),
        P("shard", None),
        P("expert", None),
        P(),
        P(("expert", "shard"), None),
        P("shard", "expert", None),
        P(("expert", "shard"), None),
        P("shard", "expert", None),
        P(),
        P("expert", None, "shard"),
        P("expert", None, "shard"),
        P("expert", "shard", None),
    )
    return jax.shard_map(
        local,
        mesh=mesh,
        in_specs=placed,
        out_specs=(P(("expert", "shard"), None), P("shard", "expert", None)),
        check_vma=False,
    )
```

profile of v0, /device:TPU:0, one launch (start us, length us, event | category | flops | bytes accessed | tf_op | source)
XLA Modules:
  0.0 599.9 jit_solution(9120764802494427658)
XLA Ops:
  7.2 0.7 fusion.44
  7.9 0.8 reshape.189
  8.7 0.8 iota_compare_fusion
  9.5 40.6 %gather_fusion = bf16[4096,16,256]{2,1,0:T(8,128)(2,1)} fusion(bf16[1056,16,256]{2,1,0:T(8,128)(2,1)} %bitcast.140, s32[4096]{0:T(1024)S(1)} %fusion.44), kind=kCustom, calls=%fused_computation | custom fusion | bytes 67125248 | tf_op jit(solution)/shard_map/gather | solution.py:14
  50.1 8.0 %fusion.24 = f32[32,2048,4]{1,2,0:T(4,128)S(1)} fusion(bf16[32,4,128]{2,1,0:T(4,128)(2,1)S(1)} %reshape.189, bf16[1,32,2048,256]{3,2,1,0:T(8,128)(2,1)} %bitcast.141), kind=kOutput, calls=%fused_computation.28 | convolution fusion | flops 67371008 | bytes 17858560 | tf_op jit(solution)/shard_map/rkgd,krtd->rkgt/dot_general | solution.py:15
  58.1 1.1 fusion.48
  59.3 7.2 %fusion.27 = bf16[32,4,128]{2,1,0:T(4,128)(2,1)S(1)} fusion(bf16[1,32,2048,256]{3,2,1,0:T(8,128)(2,1)} %bitcast.142, bf16[32,4,2048]{2,1,0:T(4,128)(2,1)S(1)} %get-tuple-element.5, f32[32,4]{1,0:T(8,128)S(1)} %get-tuple-element.4), kind=kOutput, calls=%fused_computation.36 | convolution fusion | flops 67141632 | bytes 17334784 | tf_op jit(solution)/shard_map/rkgt,krtd->rkgd/dot_general | solution.py:25
  66.5 1.5 convolution_convert_fusion.1
  68.1 0.1 select_reduce_fusion.3
  68.3 0.1 pad_add_fusion
  68.3 0.1 select_reduce_fusion.2
  68.4 0.1 copy.38
  68.5 0.1 eq.61
  68.7 0.1 fusion.40
  68.8 0.2 reduce_window_sum.11
  68.9 0.2 select_reduce_fusion.1
  69.1 0.1 reduce_sum.62
  69.3 0.6 dynamic-slice
  70.6 0.1 fusion.38
  70.7 73.8 %all-reduce.3.cloned.1.call-done = bf16[32,4096]{1,0:T(8,128)(2,1)} async-done(((bf16[32,4096]{1,0:T(8,128)(2,1)}), bf16[32,4096]{1,0:T(8,128)(2,1)}) %all-reduce.3.cloned.1.call-update) | async-done | bytes 262160
  144.5 0.9 fusion.39
  145.4 0.2 fusion.28
  145.6 0.5 convolution_convert_fusion
  146.1 0.4 reshape.192
  146.6 18.4 %all_to_all.10 = bf16[8,1,18,4096]{3,2,1,0:T(8,128)(2,1)S(1)} all-to-all(bf16[8,1,18,4096]{3,2,1,0:T(8,128)(2,1)S(1)} %bitcast.145), channel_id=1, replica_groups=mesh['expert'=8,'shard'=16] {'expert'}, dimensions={0} | all-to-all | bytes 2359296 | tf_op jit(solution)/shard_map/all_to_all | solution.py:90
  165.0 1.7 copy.41
  166.7 0.2 reduce-scatter.2.cloned.1.call-start
  166.9 119.6 %all-gather.3.cloned.1.call-done = bf16[128,1,18,4096]{3,0,2,1:T(8,128)(2,1)} async-done(((bf16[8,1,18,4096]{3,0,2,1:T(8,128)(2,1)}), bf16[128,1,18,4096]{3,0,2,1:T(8,128)(2,1)}) %all-gather.3.cloned.1.call-update) | async-done | bytes 18874384 | tf_op jit(solution)/shard_map/all_gather | solution.py:91
  286.6 16.0 %copy.42 = bf16[128,1,18,4096]{3,2,0,1:T(8,128)(2,1)S(1)} copy(bf16[128,1,18,4096]{3,0,2,1:T(8,128)(2,1)} %all-gather.3.cloned.1.call-done) | data formatting | bytes 37748736 | tf_op jit(solution)/shard_map/all_gather | solution.py:91
  302.6 8.3 %copy-done = bf16[128,1,18,4096]{3,2,0,1:T(8,128)(2,1)} copy-done((bf16[128,1,18,4096]{3,2,0,1:T(8,128)(2,1)}, bf16[128,1,18,4096]{3,2,0,1:T(8,128)(2,1)S(1)}, u32[]{:S(2)}) %copy-start) | copy-done | bytes 18874392
  310.9 17.8 %fusion.12 = f32[16,8,18,512]{3,2,1,0:T(8,128)} fusion(bf16[16,8,18,4096]{3,2,1,0:T(8,128)(2,1)S(1)} %bitcast.143, bf16[1,4096,512]{2,1,0:T(8,128)(2,1)} %param.29), kind=kOutput, calls=%fused_computation.20 | convolution fusion | flops 9663676416 | bytes 27787264 | tf_op jit(solution)/shard_map/sgkcd,kdf->sgkcf/dot_general | solution.py:92
  328.7 19.8 %fusion.64 = bf16[16,8,18,512]{3,2,1,0:T(8,128)(2,1)} fusion(bf16[16,8,18,4096]{3,2,1,0:T(8,128)(2,1)} %bitcast.144, bf16[1,4096,512]{2,1,0:T(8,128)(2,1)} %param.30, f32[16,8,18,512]{3,2,1,0:T(8,128)} %fusion.12), kind=kOutput, calls=%fused_computation.22.clone.1 | convolution fusion | flops 9670754304 | bytes 30146560 | tf_op jit(solution)/shard_map/sgkcd,kdf->sgkcf/dot_general | solution.py:93
  348.4 20.6 %convert_bitcast_fusion = bf16[16,8,1,18,4096]{4,3,1,0,2:T(8,128)(2,1)} fusion(bf16[1,512,4096]{2,1,0:T(8,128)(2,1)} %param.31, bf16[16,8,18,512]{3,2,1,0:T(8,128)(2,1)} %fusion.64), kind=kOutput, calls=%fused_computation.3 | convolution fusion | flops 9673113600 | bytes 25427968 | tf_op jit(solution)/shard_map/sgkcf,kfd->sgkcd/dot_general | solution.py:95
  369.0 188.4 %reduce-scatter.2.cloned.1.call-done = bf16[1,8,1,18,4096]{4,3,1,0,2:T(8,128)(2,1)} async-done(((bf16[16,8,1,18,4096]{4,3,1,0,2:T(8,128)(2,1)}), bf16[1,8,1,18,4096]{4,3,1,0,2:T(8,128)(2,1)}) %reduce-scatter.2.cloned.1.call-update) | async-done | bytes 1179664 | tf_op jit(solution)/shard_map/reduce_scatter | solution.py:96
  557.4 4.4 all-to-all-start.1
  561.8 0.1 reduce_sum.64
  562.0 0.1 copy.45
  562.1 0.2 reshape.212
  562.3 0.1 pad_maximum_fusion.2
  562.4 0.1 copy.37
  562.5 21.8 %all-to-all-done.1 = bf16[8,1,18,4096]{3,2,1,0:T(8,128)(2,1)S(1)} async-done(((bf16[8,1,18,4096]{3,2,1,0:T(8,128)(2,1)}), bf16[8,1,18,4096]{3,2,1,0:T(8,128)(2,1)S(1)}, u32[]{:S(2)}, u32[]{:S(2)}) %all-to-all-start.1) | async-done | bytes 1179680 | tf_op jit(solution)/shard_map/all_to_all | solution.py:103
  584.3 0.4 reshape.198
  584.7 2.2 gather_fusion.1
  586.9 2.4 reshape.224
  589.3 3.1 multiply_reduce_fusion
  592.4 0.1 fusion.31
  592.6 0.7 slice_bitcast_fusion.10
  593.3 0.1 copy-done.3
  (35 shorter events, 0.4 us)
Async XLA Ops:
  7.2 137.3 %all-reduce.3.cloned.1.call-start = ((), (), s32[]{:S(2)}) async-start(), calls=%async_computation.5 | async-start | bytes 524288
  59.2 7.3 %copy-start.2 = (bf16[512,4096]{1,0:T(8,128)(2,1)S(1)}, bf16[512,4096]{1,0:T(8,128)(2,1)}, u32[]{:S(2)}) copy-start(bf16[512,4096]{1,0:T(8,128)(2,1)} %param.22) | copy-start | bytes 12582916
  59.2 8.9 %copy-start.10 = (s32[8]{0:T(128)S(1)}, s32[8]{0:T(128)}, u32[]{:S(2)}) copy-start(s32[8]{0:T(128)} %param.28) | copy-start | bytes 100
  59.2 9.0 %copy-start.6 = (s32[1,4,2]{1,2,0:T(2,128)S(1)}, s32[1,4,2]{1,2,0:T(2,128)}, u32[]{:S(2)}) copy-start(s32[1,4,2]{1,2,0:T(2,128)} %param.25) | copy-start | bytes 100
  59.2 9.0 %copy-start.7 = (s32[60,2]{0,1:T(2,128)S(1)}, s32[60,2]{0,1:T(2,128)}, u32[]{:S(2)}) copy-start(s32[60,2]{0,1:T(2,128)} %param.24) | copy-start | bytes 1444
  59.2 10.1 %copy-start.11 = (u32[128]{0:T(128)S(1)}, u32[128]{0:T(128)}, u32[]{:S(2)}) copy-start(u32[128]{0:T(128)} %constant.45) | copy-start | bytes 1540
  59.3 85.2 %copy-start.4 = (bf16[1,4,4096]{2,1,0:T(4,128)(2,1)S(1)}, bf16[1,4,4096]{2,1,0:T(4,128)(2,1)}, u32[]{:S(2)}) copy-start(bf16[1,4,4096]{2,1,0:T(4,128)(2,1)} %param.17) | copy-start | bytes 98308
  59.3 86.1 %copy-start.1 = (bf16[60,4096]{1,0:T(8,128)(2,1)S(1)}, bf16[60,4096]{1,0:T(8,128)(2,1)}, u32[]{:S(2)}) copy-start(bf16[60,4096]{1,0:T(8,128)(2,1)} %param.16) | copy-start | bytes 1474564
  59.3 86.3 %copy-start.5 = (f32[4096]{0:T(1024)S(1)}, f32[4096]{0:T(1024)}, u32[]{:S(2)}) copy-start(f32[4096]{0:T(1024)} %param.23) | copy-start | bytes 49156
  68.1 218.5 %all-gather.3.cloned.1.call-start = ((), (), s32[]{:S(2)}) async-start(), calls=%async_computation.4 | async-start | bytes 20054016 | tf_op jit(solution)/shard_map/all_gather | solution.py:91
  166.7 390.7 %reduce-scatter.2.cloned.1.call-start = ((), (), s32[]{:S(2)}) async-start(), calls=%async_computation.3 | async-start | bytes 26738688 | tf_op jit(solution)/shard_map/reduce_scatter | solution.py:96
  302.6 8.3 %copy-start = (bf16[128,1,18,4096]{3,2,0,1:T(8,128)(2,1)}, bf16[128,1,18,4096]{3,2,0,1:T(8,128)(2,1)S(1)}, u32[]{:S(2)}) copy-start(bf16[128,1,18,4096]{3,2,0,1:T(8,128)(2,1)S(1)} %copy.42) | copy-start | bytes 56623108
  369.0 193.3 %copy-start.8 = (f32[1,4,2]{1,2,0:T(2,128)S(1)}, f32[1,4,2]{1,2,0:T(2,128)}, u32[]{:S(2)}) copy-start(f32[1,4,2]{1,2,0:T(2,128)} %param.27) | copy-start | bytes 100
  369.0 193.3 %copy-start.9 = (f32[60,2]{0,1:T(2,128)S(1)}, f32[60,2]{0,1:T(2,128)}, u32[]{:S(2)}) copy-start(f32[60,2]{0,1:T(2,128)} %param.26) | copy-start | bytes 1444
  557.4 26.9 %all-to-all-start.1 = ((bf16[8,1,18,4096]{3,2,1,0:T(8,128)(2,1)}), bf16[8,1,18,4096]{3,2,1,0:T(8,128)(2,1)S(1)}, u32[]{:S(2)}, u32[]{:S(2)}) async-start(bf16[8,1,18,4096]{3,2,1,0:T(8,128)(2,1)} %bitcast.146), calls=%async_computation.2 | async-start | bytes 3145728 | tf_op jit(solution)/shard_map/all_to_all | solution.py:103
  592.6 0.8 copy-start.3
Sparse Core Ops, SparseCore 0:
  68.2 76.2 all-reduce.2
  166.8 119.6 all-gather.2
  369.2 188.1 reduce-scatter.1
where the time goes:
time: 601 us; the launch traced here: 600 us
  waiting for transfers between devices  404 us (67%)
  matrix products  75.5 us (13%)
  local copies, waits for them, and re-layouts  75.2 us (13%)
  blocking collectives  18.4 us (3%)
  between operations  14.7 us (2%)
  other arithmetic  7.84 us (1%)
    reduce_scatter x1, waiting for transfers between devices, local(): lax.psum_scatter(term.astype(jnp.bfloat16).astype(jnp.float32).astype(jnp...  188 us
    all_gather x1, waiting for transfers between devices, local(): piece_rows = lax.all_gather(received[None], 'shard', axis=0, tiled=True)  120 us
    unnamed x4, waiting for transfers between devices  73.8 us
    gather x1, local copies, waits for them, and re-layouts, table_attention(): kv_pool[:, page_rows].reshape(kv_local, dec_dev, span_tokens, twice_dim)  40.6 us
    all_to_all x1, waiting for transfers between devices, local(): lax.all_to_all(outputs, 'expert', split_axis=0, concat_axis=0, tiled=True)  21.8 us
    dot_general x1, matrix products, local(): jnp.einsum('sgkcf,kfd->sgkcd', act, w_down, preferred_element_type=jnp.fl...  20.6 us
    dot_general x1, matrix products, local(): jnp.einsum('sgkcd,kdf->sgkcf', piece_rows, w_up, preferred_element_type=j...  19.8 us
    all_to_all x1, blocking collectives, local(): lax.all_to_all(buffer, 'expert', split_axis=0, concat_axis=0, tiled=True)  18.4 us
  transfers between devices with their start and end apart: 4, of which 4 were waited for; matrix products, arithmetic and copies ran while one was open for 0% of the time, Pallas kernels for 0%

commit v1 on v0

--- a/solution.py
+++ b/solution.py
@@ -88,7 +88,9 @@
     buffer = jnp.dot(placing, normed, preferred_element_type=jnp.float32).astype(jnp.bfloat16)
     buffer = buffer.reshape(n_expert, per_group, slot_cap, width)
     received = lax.all_to_all(buffer, "expert", split_axis=0, concat_axis=0, tiled=True)
-    piece_rows = lax.all_gather(received[None], "shard", axis=0, tiled=True)
+    piece_rows = jnp.concatenate(
+        lax.all_to_all(jnp.stack([received[None]] * lax.axis_size("shard")), "shard", 0, 0), axis=0
+    )
     gate = jnp.einsum("sgkcd,kdf->sgkcf", piece_rows, w_gate, preferred_element_type=jnp.float32)
     upper = jnp.einsum("sgkcd,kdf->sgkcf", piece_rows, w_up, preferred_element_type=jnp.float32)
     act = (jax.nn.silu(gate) * upper).astype(jnp.bfloat16)

time: 601 us -> 695 us (1.16)
  blocking collectives: 18.4 us -> 235 us
  waiting for transfers between devices: 404 us -> 282 us
  local copies, waits for them, and re-layouts: 75.2 us -> 52.1 us
  matrix products: 75.5 us -> 92.7 us
    all_to_all x0 -> x1, blocking collectives: none -> 217 us  [local(): lax.all_to_all(jnp.stack([received[None]] * lax.axis_size('shard')), 'sha...]
    all_gather x1 -> x0, waiting for transfers between devices: 120 us -> none  [local(): piece_rows = lax.all_gather(received[None], 'shard', axis=0, tiled=True)]
    all_gather x1 -> x0, local copies, waits for them, and re-layouts: 16 us -> none  [local(): piece_rows = lax.all_gather(received[None], 'shard', axis=0, tiled=True)]
    dot_general x1, matrix products: 19.8 us -> 29 us  [local(): jnp.einsum('sgkcd,kdf->sgkcf', piece_rows, w_up, preferred_element_type=j...]
    unnamed x25, local copies, waits for them, and re-layouts: 9.04 us -> 0.75 us
    dot_general x1, matrix products: 17.8 us -> 25.6 us  [local(): jnp.einsum('sgkcd,kdf->sgkcf', piece_rows, w_gate, preferred_element_type...]
    unnamed x4 -> x3, waiting for transfers between devices: 73.8 us -> 73.8 us
  transfers between devices with their start and end apart: 4 -> 3, of which waited for: 4 -> 3; matrix products, arithmetic and copies ran while one was open for 0% -> 0% of each run, Pallas kernels for 0% -> 0%
where the time goes in v1:
time: 695 us; the launch traced here: 689 us
  waiting for transfers between devices  282 us (41%)
  blocking collectives  235 us (34%)
  matrix products  92.7 us (13%)
  local copies, waits for them, and re-layouts  52.1 us (7%)
  between operations  15.2 us (2%)
  other arithmetic  7.84 us (1%)
    all_to_all x1, blocking collectives, local(): lax.all_to_all(jnp.stack([received[None]] * lax.axis_size('shard')), 'sha...  217 us
    reduce_scatter x1, waiting for transfers between devices, local(): lax.psum_scatter(term.astype(jnp.bfloat16).astype(jnp.float32).astype(jnp...  186 us
    unnamed x3, waiting for transfers between devices  73.8 us
    gather x1, local copies, waits for them, and re-layouts, table_attention(): kv_pool[:, page_rows].reshape(kv_local, dec_dev, span_tokens, twice_dim)  40.6 us
    dot_general x1, matrix products, local(): jnp.einsum('sgkcd,kdf->sgkcf', piece_rows, w_up, preferred_element_type=j...  29 us
    dot_general x1, matrix products, local(): jnp.einsum('sgkcd,kdf->sgkcf', piece_rows, w_gate, preferred_element_type...  25.6 us
    all_to_all x1, waiting for transfers between devices, local(): lax.all_to_all(outputs, 'expert', split_axis=0, concat_axis=0, tiled=True)  21.9 us
    dot_general x1, matrix products, local(): jnp.einsum('sgkcf,kfd->sgkcd', act, w_down, preferred_element_type=jnp.fl...  20.8 us
  transfers between devices with their start and end apart: 3, of which 3 were waited for; matrix products, arithmetic and copies ran while one was open for 0% of the time, Pallas kernels for 0%

profile of v1, /device:TPU:0, one launch (start us, length us, event | category | flops | bytes accessed | tf_op | source)
XLA Modules:
  0.0 688.9 jit_solution(17751042772438278228)
XLA Ops:
  7.2 0.7 fusion.54
  7.9 0.8 reshape.195
  8.7 0.8 iota_compare_fusion
  9.5 40.6 %gather_fusion = bf16[4096,16,256]{2,1,0:T(8,128)(2,1)} fusion(bf16[1056,16,256]{2,1,0:T(8,128)(2,1)} %bitcast.149, s32[4096]{0:T(1024)S(1)} %fusion.54), kind=kCustom, calls=%fused_computation | custom fusion | bytes 67125248 | tf_op jit(solution)/shard_map/gather | solution.py:14
  50.1 8.0 %fusion.34 = f32[32,2048,4]{1,2,0:T(4,128)S(1)} fusion(bf16[32,4,128]{2,1,0:T(4,128)(2,1)S(1)} %reshape.195, bf16[1,32,2048,256]{3,2,1,0:T(8,128)(2,1)} %bitcast.150), kind=kOutput, calls=%fused_computation.32 | convolution fusion | flops 67371008 | bytes 17858560 | tf_op jit(solution)/shard_map/rkgd,krtd->rkgt/dot_general | solution.py:15
  58.1 1.1 fusion.58
  59.3 7.2 %fusion.37 = bf16[32,4,128]{2,1,0:T(4,128)(2,1)S(1)} fusion(bf16[1,32,2048,256]{3,2,1,0:T(8,128)(2,1)} %bitcast.151, bf16[32,4,2048]{2,1,0:T(4,128)(2,1)S(1)} %get-tuple-element.5, f32[32,4]{1,0:T(8,128)S(1)} %get-tuple-element.4), kind=kOutput, calls=%fused_computation.40 | convolution fusion | flops 67141632 | bytes 17334784 | tf_op jit(solution)/shard_map/rkgt,krtd->rkgd/dot_general | solution.py:25
  66.5 1.5 convolution_convert_fusion.1
  68.1 0.1 select_reduce_fusion.3
  68.2 0.1 pad_add_fusion
  68.3 0.1 select_reduce_fusion.2
  68.4 0.1 copy.38
  68.5 0.1 eq.61
  68.7 0.1 fusion.50
  68.7 0.2 reduce_window_sum.11
  68.9 0.2 select_reduce_fusion.1
  69.1 0.1 reduce_sum.62
  69.2 0.1 copy.39
  69.3 0.6 dynamic-slice
  70.6 0.1 fusion.48
  70.7 73.8 %all-reduce.3.cloned.1.call-done = bf16[32,4096]{1,0:T(8,128)(2,1)} async-done(((bf16[32,4096]{1,0:T(8,128)(2,1)}), bf16[32,4096]{1,0:T(8,128)(2,1)}) %all-reduce.3.cloned.1.call-update) | async-done | bytes 262160
  144.5 0.9 fusion.49
  145.3 0.2 fusion.38
  145.6 0.5 convolution_convert_fusion
  146.1 0.4 reshape.198
  146.6 18.4 %all_to_all.18 = bf16[8,1,18,4096]{3,2,1,0:T(8,128)(2,1)S(1)} all-to-all(bf16[8,1,18,4096]{3,2,1,0:T(8,128)(2,1)S(1)} %bitcast.152), channel_id=1, replica_groups=mesh['expert'=8,'shard'=16] {'expert'}, dimensions={0} | all-to-all | bytes 2359296 | tf_op jit(solution)/shard_map/all_to_all | solution.py:90
  165.0 0.7 copy.41
  165.6 2.2 stack.9
  167.9 216.6 %all_to_all.19 = bf16[16,1,8,1,18,4096]{5,2,4,3,1,0:T(8,128)(2,1)} all-to-all(bf16[16,1,8,1,18,4096]{5,2,4,3,1,0:T(8,128)(2,1)S(1)} %stack.9), channel_id=1, replica_groups=mesh['expert'=8,'shard'=16] {'shard'}, dimensions={0} | all-to-all | bytes 37748736 | tf_op jit(solution)/shard_map/all_to_all | solution.py:92
  384.5 25.6 %fusion.3 = f32[16,8,18,512]{3,2,1,0:T(8,128)} fusion(bf16[16,1,8,1,18,4096]{5,2,4,3,1,0:T(8,128)(2,1)} %all_to_all.19, bf16[1,4096,512]{2,1,0:T(8,128)(2,1)S(1)} %copy-done.9), kind=kOutput, calls=%fused_computation.5 | convolution fusion | flops 9663676416 | bytes 27787264 | tf_op jit(solution)/shard_map/sgkcd,kdf->sgkcf/dot_general | solution.py:94
  410.1 29.0 %fusion.72 = bf16[16,8,18,512]{3,2,1,0:T(8,128)(2,1)} fusion(bf16[1,4096,512]{2,1,0:T(8,128)(2,1)} %param.30, bf16[16,1,8,1,18,4096]{5,2,4,3,1,0:T(8,128)(2,1)} %all_to_all.19, f32[16,8,18,512]{3,2,1,0:T(8,128)} %fusion.3), kind=kOutput, calls=%fused_computation.26.clone.1 | convolution fusion | flops 9670754304 | bytes 30146560 | tf_op jit(solution)/shard_map/sgkcd,kdf->sgkcf/dot_general | solution.py:95
  439.1 20.8 %convert_bitcast_fusion = bf16[16,8,1,18,4096]{4,3,1,0,2:T(8,128)(2,1)} fusion(bf16[1,512,4096]{2,1,0:T(8,128)(2,1)} %param.31, bf16[16,8,18,512]{3,2,1,0:T(8,128)(2,1)} %fusion.72), kind=kOutput, calls=%fused_computation.9 | convolution fusion | flops 9673113600 | bytes 25427968 | tf_op jit(solution)/shard_map/sgkcf,kfd->sgkcd/dot_general | solution.py:97
  459.9 185.9 %reduce-scatter.2.cloned.1.call-done = bf16[1,8,1,18,4096]{4,3,1,0,2:T(8,128)(2,1)} async-done(((bf16[16,8,1,18,4096]{4,3,1,0,2:T(8,128)(2,1)}), bf16[1,8,1,18,4096]{4,3,1,0,2:T(8,128)(2,1)}) %reduce-scatter.2.cloned.1.call-update) | async-done | bytes 1179664 | tf_op jit(solution)/shard_map/reduce_scatter | solution.py:98
  645.8 4.4 all-to-all-start.2
  650.2 0.1 reduce_sum.64
  650.3 0.1 copy.44
  650.4 0.1 copy.45
  650.5 0.2 reshape.218
  650.7 0.1 pad_maximum_fusion.2
  650.8 0.1 copy.37
  650.9 21.9 %all-to-all-done.2 = bf16[8,1,18,4096]{3,2,1,0:T(8,128)(2,1)S(1)} async-done(((bf16[8,1,18,4096]{3,2,1,0:T(8,128)(2,1)}), bf16[8,1,18,4096]{3,2,1,0:T(8,128)(2,1)S(1)}, u32[]{:S(2)}, u32[]{:S(2)}) %all-to-all-start.2) | async-done | bytes 1179680 | tf_op jit(solution)/shard_map/all_to_all | solution.py:105
  672.8 0.4 reshape.204
  673.2 2.2 gather_fusion.1
  675.4 2.4 reshape.228
  677.7 3.1 multiply_reduce_fusion
  680.9 0.1 fusion.41
  681.0 0.7 slice_bitcast_fusion.10
  681.7 0.1 copy-done.2
  (33 shorter events, 0.2 us)
Async XLA Ops:
  7.2 137.3 %all-reduce.3.cloned.1.call-start = ((), (), s32[]{:S(2)}) async-start(), calls=%async_computation.5 | async-start | bytes 524288
  59.2 7.3 %copy-start.1 = (bf16[512,4096]{1,0:T(8,128)(2,1)S(1)}, bf16[512,4096]{1,0:T(8,128)(2,1)}, u32[]{:S(2)}) copy-start(bf16[512,4096]{1,0:T(8,128)(2,1)} %param.22) | copy-start | bytes 12582916
  59.2 8.9 %copy-start.10 = (s32[8]{0:T(128)S(1)}, s32[8]{0:T(128)}, u32[]{:S(2)}) copy-start(s32[8]{0:T(128)} %param.28) | copy-start | bytes 100
  59.2 9.0 %copy-start.5 = (s32[1,4,2]{1,2,0:T(2,128)S(1)}, s32[1,4,2]{1,2,0:T(2,128)}, u32[]{:S(2)}) copy-start(s32[1,4,2]{1,2,0:T(2,128)} %param.25) | copy-start | bytes 100
  59.2 9.0 %copy-start.6 = (s32[60,2]{0,1:T(2,128)S(1)}, s32[60,2]{0,1:T(2,128)}, u32[]{:S(2)}) copy-start(s32[60,2]{0,1:T(2,128)} %param.24) | copy-start | bytes 1444
  59.2 10.1 %copy-start.11 = (u32[128]{0:T(128)S(1)}, u32[128]{0:T(128)}, u32[]{:S(2)}) copy-start(u32[128]{0:T(128)} %constant.45) | copy-start | bytes 1540
  59.3 85.2 %copy-start.3 = (bf16[1,4,4096]{2,1,0:T(4,128)(2,1)S(1)}, bf16[1,4,4096]{2,1,0:T(4,128)(2,1)}, u32[]{:S(2)}) copy-start(bf16[1,4,4096]{2,1,0:T(4,128)(2,1)} %param.17) | copy-start | bytes 98308
  59.3 86.1 %copy-start = (bf16[60,4096]{1,0:T(8,128)(2,1)S(1)}, bf16[60,4096]{1,0:T(8,128)(2,1)}, u32[]{:S(2)}) copy-start(bf16[60,4096]{1,0:T(8,128)(2,1)} %param.16) | copy-start | bytes 1474564
  59.3 86.3 %copy-start.4 = (f32[4096]{0:T(1024)S(1)}, f32[4096]{0:T(1024)}, u32[]{:S(2)}) copy-start(f32[4096]{0:T(1024)} %param.23) | copy-start | bytes 49156
  68.1 577.8 %reduce-scatter.2.cloned.1.call-start = ((), (), s32[]{:S(2)}) async-start(), calls=%async_computation.4 | async-start | bytes 26738688 | tf_op jit(solution)/shard_map/reduce_scatter | solution.py:98
  167.9 216.6 %copy-start.9 = (bf16[1,4096,512]{2,1,0:T(8,128)(2,1)S(1)}, bf16[1,4096,512]{2,1,0:T(8,128)(2,1)}, u32[]{:S(2)}) copy-start(bf16[1,4096,512]{2,1,0:T(8,128)(2,1)} %param.29) | copy-start | bytes 12582916
  459.9 190.8 %copy-start.7 = (f32[1,4,2]{1,2,0:T(2,128)S(1)}, f32[1,4,2]{1,2,0:T(2,128)}, u32[]{:S(2)}) copy-start(f32[1,4,2]{1,2,0:T(2,128)} %param.27) | copy-start | bytes 100
  459.9 190.8 %copy-start.8 = (f32[60,2]{0,1:T(2,128)S(1)}, f32[60,2]{0,1:T(2,128)}, u32[]{:S(2)}) copy-start(f32[60,2]{0,1:T(2,128)} %param.26) | copy-start | bytes 1444
  645.8 26.9 %all-to-all-start.2 = ((bf16[8,1,18,4096]{3,2,1,0:T(8,128)(2,1)}), bf16[8,1,18,4096]{3,2,1,0:T(8,128)(2,1)S(1)}, u32[]{:S(2)}, u32[]{:S(2)}) async-start(bf16[8,1,18,4096]{3,2,1,0:T(8,128)(2,1)} %bitcast.154), calls=%async_computation.3 | async-start | bytes 3145728 | tf_op jit(solution)/shard_map/all_to_all | solution.py:105
  681.0 0.8 copy-start.2
Sparse Core Ops, SparseCore 0:
  68.2 76.2 all-reduce.2
  460.0 185.7 reduce-scatter.1
